TPU v7x, 256 devices: a whole 4x4x8 slice. The times are simulated.
256 devices in a mesh: dp: 64 (over z_hi, y, x), tensor: 4 (over z_lo, core).
Axes of the slice: x: 4, y: 4, z: 8 (z_hi: 4, z_lo: 2; z = z_hi * 2 + z_lo), core: 2. Of those that a mesh axis runs over, the one named last changes fastest.
Arguments:
- hidden: bfloat16 [32768, 8192], P('dp', 'tensor'), may hold values from -16 to 16
- kv_weight: bfloat16 [8192, 1024], P(None, 'tensor'), may hold values from -0.0625 to 0.0625
- queries: bfloat16 [32768, 4096], P('dp', 'tensor'), may hold values from -28 to 28
- out_grad: bfloat16 [32768, 4096], P('dp', 'tensor'), may hold values from -6 to 6
- live_blocks: int32 [64], P('dp'), may hold values from 0 to 4, as said below
- doc_start: int32 [32768], P('dp'), may hold values from 0 to 127, as said below
Outputs:
- q_grad: bfloat16 [32768, 4096], P('dp', 'tensor')
- hidden_grad: bfloat16 [32768, 8192], P('dp', 'tensor')
- kv_weight_grad: float32 [8192, 1024], P('dp', 'tensor')
Inputs may be any that keep to these rules, and one draw needn't show every extreme that they name: live_blocks[i] + live_blocks[j] = 4 for the two indices i and j of dp that lie half the axis apart; the live blocks of an index are its first ones. doc_start of a row is at most its own position within its block, position 0 of every block is 0, and the rows of one document are consecutive.
All inputs are finite; a program needn't handle non-finite values.
Results may differ from a plain program's by a relative error of at most 0.014.
The roundings to bfloat16 on the way count: a program that leaves them out, or rounds other values in their place, can miss the bound.
Values may be sent and summed in bfloat16 or wider, within the bound.
A program may use at most 128 MiB of HBM per device.

v0:
```python
import jax
import jax.numpy as jnp
from jax import lax
from jax.sharding import PartitionSpec as P

HEAD_DIM = 128
BLOCK = 128
NBLK = 4


def attend(query_rows, key_rows, value_rows, grad_rows, start_rows, live_slots):
    factor = HEAD_DIM ** (-0.5)
    position = jnp.arange(BLOCK)
    allowed = (
        (position[None, None, :] >= start_rows[:, :, None])
        & (position[None, None, :] <= position[None, :, None])
        & live_slots[:, None, None]
    )
    allowed = allowed[:, None, None]
    scores = (
        jnp.einsum("brkgd,bskd->bkgrs", query_rows, key_rows, preferred_element_type=jnp.float32)
        * factor
    )
    row_max = jnp.max(jnp.where(allowed, scores, -1e30), axis=-1, keepdims=True)
    weights = jnp.where(allowed, jnp.exp(scores - row_max), 0.0)
    row_sum = jnp.sum(weights, axis=-1, keepdims=True)
    row_sum = jnp.where(live_slots[:, None, None, None, None], row_sum, 1.0)
    prob_full = weights / row_sum
    prob_low = prob_full.astype(jnp.bfloat16)
    attended = jnp.einsum(
        "bkgrs,bskd->brkgd", prob_low, value_rows, preferred_element_type=jnp.float32
    ).astype(jnp.bfloat16)
    attended = lax.optimization_barrier(attended)
    row_dot = jnp.sum(grad_rows.astype(jnp.float32) * attended.astype(jnp.float32), axis=-1)
    prob_grad = jnp.einsum(
        "brkgd,bskd->bkgrs", grad_rows, value_rows, preferred_element_type=jnp.float32
    )
    score_grad = (
        prob_full * (prob_grad - jnp.transpose(row_dot, (0, 2, 3, 1))[..., None]) * factor
    ).astype(jnp.bfloat16)
    query_grad = jnp.einsum(
        "bkgrs,bskd->brkgd", score_grad, key_rows, preferred_element_type=jnp.float32
    ).astype(jnp.bfloat16)
    key_grad = jnp.einsum(
        "bkgrs,brkgd->bskd", score_grad, query_rows, preferred_element_type=jnp.float32
    ).astype(jnp.bfloat16)
    value_grad = jnp.einsum(
        "bkgrs,brkgd->bskd", prob_low, grad_rows, preferred_element_type=jnp.float32
    ).astype(jnp.bfloat16)
    return (query_grad, jnp.stack([key_grad, value_grad], axis=3))


def on_device(hidden, kv_weight, queries, out_grad, live_blocks, doc_start):
    row_count = hidden.shape[0]
    kv_cols = kv_weight.shape[1]
    kv_local = kv_cols // (2 * HEAD_DIM)
    group_size = queries.shape[1] // (kv_local * HEAD_DIM)
    gathered = lax.all_gather(hidden, "tensor", axis=1, tiled=True)
    key_value = jnp.dot(gathered, kv_weight, preferred_element_type=jnp.float32).astype(
        jnp.bfloat16
    )
    key_value = key_value.reshape(NBLK, BLOCK, kv_local, 2, HEAD_DIM)
    key_rows = key_value[:, :, :, 0]
    value_rows = key_value[:, :, :, 1]
    query_rows = queries.reshape(NBLK, BLOCK, kv_local, group_size, HEAD_DIM)
    grad_rows = out_grad.reshape(NBLK, BLOCK, kv_local, group_size, HEAD_DIM)
    start_rows = doc_start.reshape(NBLK, BLOCK)
    live_count = live_blocks[0]
    query_grad, kv_grad = attend(
        query_rows, key_rows, value_rows, grad_rows, start_rows, jnp.arange(NBLK) < live_count
    )
    q_grad = query_grad.reshape(row_count, queries.shape[1])
    kv_grad = kv_grad.reshape(row_count, kv_cols)
    partial_value = lax.dot_general(
        kv_grad, kv_weight, (((1,), (1,)), ((), ())), preferred_element_type=jnp.float32
    )
    hidden_grad = lax.psum_scatter(
        partial_value.astype(jnp.bfloat16), "tensor", scatter_dimension=1, tiled=True
    )
    weight_grad = lax.psum_scatter(
        lax.dot_general(
            gathered, kv_grad, (((0,), (0,)), ((), ())), preferred_element_type=jnp.float32
        ),
        "dp",
        scatter_dimension=0,
        tiled=True,
    )
    return (q_grad, hidden_grad, weight_grad)


def solution(mesh):
    in_specs = (
        P("dp", "tensor"),
        P(None, "tensor"),
        P("dp", "tensor"),
        P("dp", "tensor"),
        P("dp"),
        P("dp"),
    )
    out_specs = (P("dp", "tensor"), P("dp", "tensor"), P("dp", "tensor"))
    return jax.shard_map(
        on_device, mesh=mesh, in_specs=in_specs, out_specs=out_specs, check_vma=False
    )
```

profile of v0, /device:TPU:1, one launch (start us, length us, event | category | flops | bytes accessed | tf_op | source)
XLA Modules:
  0.0 614.5 jit_solution(17390597814734032298)
XLA Ops:
  7.2 0.7 all-gather.2.cloned.1.call-update
  8.9 1.2 copy.49
  10.4 1.8 copy.50
  12.2 1.9 copy.26
  14.3 83.8 %all-gather.2.cloned.1.call-done = bf16[512,8192]{1,0:T(8,128)(2,1)} async-done(((bf16[512,2048]{1,0:T(8,128)(2,1)}), bf16[512,8192]{1,0:T(8,128)(2,1)}) %all-gather.2.cloned.1.call-update) | async-done | bytes 8388624 | tf_op jit(solution)/shard_map/all_gather | solution.py:58
  98.0 7.6 %convolution_convert_fusion.3 = bf16[512,256]{1,0:T(8,128)(2,1)} fusion(bf16[512,8192]{1,0:T(8,128)(2,1)} %all-gather.2.cloned.1.call-done, bf16[8192,256]{1,0:T(8,128)(2,1)} %param.7), kind=kOutput, calls=%fused_computation.20 | convolution fusion | flops 2147614720 | bytes 12845056 | tf_op jit(solution)/shard_map/dot_general | solution.py:59
  105.7 1.0 reshape.122
  107.1 0.5 fusion.3
  107.6 0.5 fusion.7
  108.4 0.7 fusion.13
  109.1 0.8 fusion.8
  110.3 0.9 fusion.10
  111.3 0.4 fusion.14
  112.0 0.5 slice-done
  112.5 1.3 slice-done.1
  113.8 5.8 convolution_bitcast_fusion
  119.8 7.8 %convolution_convert_fusion = bf16[512,8192]{1,0:T(8,128)(2,1)} fusion(bf16[8192,256]{1,0:T(8,128)(2,1)} %param.7, bf16[64,8,2,128]{3,2,1,0:T(2,128)(2,1)S(1)} %bitcast.155), kind=kOutput, calls=%fused_computation | convolution fusion | flops 2151677952 | bytes 12845056 | tf_op jit(solution)/shard_map/dot_general | solution.py:74
  127.6 0.9 copy-done.4
  128.6 0.5 fusion.9
  129.1 0.7 copy.29
  129.8 1.2 copy.80
  131.0 353.3 %reduce-scatter.5.cloned.1.call-done = f32[128,256]{0,1:T(8,128)} async-done(((f32[8192,256]{0,1:T(8,128)}), f32[128,256]{0,1:T(8,128)}) %reduce-scatter.5.cloned.1.call-update) | async-done | bytes 131088 | tf_op jit(solution)/shard_map/reduce_scatter | solution.py:80
  484.4 1.7 copy.33
  486.0 122.0 %reduce-scatter.3.cloned.1.call-done = bf16[512,2048]{1,0:T(8,128)(2,1)} async-done(((bf16[512,8192]{1,0:T(8,128)(2,1)}), bf16[512,2048]{1,0:T(8,128)(2,1)}) %reduce-scatter.3.cloned.1.call-update) | async-done | bytes 2097168 | tf_op jit(solution)/shard_map/reduce_scatter | solution.py:77
  (29 shorter events, 2.3 us)
Async XLA Ops:
  7.2 1.4 copy-start.1
  7.2 1.7 copy-start
  7.2 90.9 %all-gather.2.cloned.1.call-start = ((), (), s32[]{:S(2)}) async-start(), calls=%async_computation.2 | async-start | bytes 10485760 | tf_op jit(solution)/shard_map/all_gather | solution.py:58
  7.9 476.4 %reduce-scatter.5.cloned.1.call-start = ((), (), s32[]{:S(2)}) async-start(), calls=%async_computation.4 | async-start | bytes 8519680 | tf_op jit(solution)/shard_map/reduce_scatter | solution.py:80
  12.2 2.0 copy-start.5
  107.0 1.0 copy-start.3
  107.1 1.3 copy-start.2
  110.3 2.2 slice-start
  110.3 3.5 slice-start.1
  119.6 488.4 %reduce-scatter.3.cloned.1.call-start = ((), (), s32[]{:S(2)}) async-start(), calls=%async_computation.3 | async-start | bytes 10485760 | tf_op jit(solution)/shard_map/reduce_scatter | solution.py:77
  127.6 0.9 copy-start.4
Sparse Core Ops, SparseCore 0:
  9.8 88.2 all-gather.1
  119.7 364.6 reduce-scatter.4
  487.6 120.4 reduce-scatter.2
where the time goes:
time: 615 us
  waiting for transfers between devices  560 us (91%)
  matrix products  25.1 us (4%)
  between operations  14.6 us (2%)
  local copies, waits for them, and re-layouts  13.5 us (2%)
    reduce_scatter x1, waiting for transfers between devices, on_device(): lax.psum_scatter(lax.dot_general(gathered, kv_grad, (((0,), (0,)), ((), (...  353 us
    reduce_scatter x1, waiting for transfers between devices, on_device(): lax.psum_scatter(partial_value.astype(jnp.bfloat16), 'tensor', scatter_di...  122 us
    all_gather x1, waiting for transfers between devices, on_device(): gathered = lax.all_gather(hidden, 'tensor', axis=1, tiled=True)  83.8 us
  transfers between devices with their start and end apart: 3, of which 3 were waited for; matrix products, arithmetic and copies ran while one was open for 3% of the time, Pallas kernels for 0%

commit v1 on v0

v1 whole, which is shorter than its diff:
```python
import jax
import jax.numpy as jnp
from jax import lax
from jax.experimental import pallas as pl
from jax.experimental.pallas import tpu as pltpu
from jax.sharding import PartitionSpec as P

BF16 = jnp.bfloat16
F32 = jnp.float32
HD = 128
ROWS = 512
NB = 4
NH = 8
KD = 2048
KC = 256
MESH = pl.DeviceIdType.MESH


def dot(a, b, dims):
    return lax.dot_general(a, b, (dims, ((), ())), preferred_element_type=F32)


def kernel(
    live_ref, start_ref, hid_hbm, w_hbm, q_hbm, g_hbm,
    qg_out, hg_out, wg_out,
    hid, hid_t, wts, qv, gv, qg, hg,
    own, pp, pf, ff, r_pp, r_pf, r_z, kvg,
    s_far, s_rt, s_lt, st_rt, st_lt, acc, r_rel, r_nbl, r_nbr,
    t_acc, q_relay, q_rel, q_nbl, q_nbr,
    z_acc, r_fin, out_v,
    loc, snd, rcv,
):
    counter = [0, 0]

    def new_sem(count=1):
        first = counter[0]
        counter[0] += count
        return first

    def new_loc():
        counter[1] += 1
        return loc.at[counter[1] - 1]

    dp = lax.axis_index("dp")
    j = lax.axis_index("tensor")
    zh = dp // 16
    y = (dp // 4) % 4
    x = dp % 4
    zl = j // 2
    c = j % 2
    pj = 2 * zl + 1 - c
    fz = 2 * (1 - zl)
    tf = fz + c
    tp = fz + 1 - c

    def dev(zh_, y_, x_, t_):
        return {"dp": zh_ * 16 + y_ * 4 + x_, "tensor": t_}

    partner = dev(zh, y, x, pj)
    pair_same = dev(zh, y, x, tf)
    pair_other = dev(zh, y, x, tp)
    zo = (zh + 2 * zl + 3) % 4
    oth_same = dev(zo, y, x, tf)
    oth_other = dev(zo, y, x, tp)
    right = (dev(zh, y, (x + 1) % 4, j), dev(zh, (y + 1) % 4, x, j))
    left = (dev(zh, y, (x + 3) % 4, j), dev(zh, (y + 3) % 4, x, j))
    me = (x, y)

    def rcopy(src, dst, sem, to):
        return pltpu.make_async_remote_copy(
            src_ref=src, dst_ref=dst, send_sem=snd.at[sem], recv_sem=rcv.at[sem],
            device_id=to, device_id_type=MESH,
        )

    cp_own = pltpu.make_async_copy(w_hbm.at[pl.ds(KD * j, KD), :], wts.at[j], new_loc())
    cp_own.start()
    cp_hid = pltpu.make_async_copy(hid_hbm, hid, new_loc())
    cp_hid.start()

    barrier = pltpu.get_barrier_semaphore()

    def greet(to):
        pl.semaphore_signal(barrier, inc=1, device_id=to, device_id_type=MESH)

    for to in (partner, pair_same, pair_other, oth_same, oth_other) + right + left:
        greet(to)
    for k in range(4):
        @pl.when(jnp.logical_not((zh == j) & (j == k)))
        def _():
            greet(dev(j, y, x, k))

        @pl.when(jnp.logical_not((zh == j) & (zh == k)))
        def _():
            greet(dev(k, y, x, zh))
    own_case = jnp.where(zh == j, 1, 0)
    pl.semaphore_wait(barrier, 17 - 2 * own_case)

    quarter = KD // 8
    cp_z = []
    for k in range(2):
        cd = (1 - c) if k == 0 else c
        td = fz + cd
        for h in range(2):
            to = ((pair_other, pair_same), (oth_other, oth_same))[h][k]
            off = 1024 * h + quarter * me[h]
            cp = rcopy(
                w_hbm.at[pl.ds(KD * td + off, quarter), :],
                wts.at[j, pl.ds(off, quarter), :], new_sem(), to,
            )
            cp.start()
            cp_z.append(cp)
    cp_pw = rcopy(w_hbm.at[pl.ds(KD * pj, KD), :], wts.at[j], new_sem(), partner)
    cp_pw.start()
    cp_q = pltpu.make_async_copy(q_hbm, qv, new_loc())
    cp_q.start()
    cp_g = pltpu.make_async_copy(g_hbm, gv, new_loc())
    cp_g.start()

    def proj(t, store):
        @pl.loop(0, 2)
        def _(n):
            rows = pl.ds(n * 256, 256)
            store(rows, dot(hid[rows, :], wts[t], ((1,), (0,))))

    def to_ref(ref):
        def store(rows, value):
            ref[rows, :] = value
        return store

    cp_hid.wait()
    cp_own.wait()
    proj(j, to_ref(own))

    ring = []
    for k in range(2):
        ts = (tp, tf)[k]
        for h in range(2):
            cp_z[2 * k + h].wait_recv()
            sems = [new_sem() for _ in range(4)]

            def piece(origin, lo, size, h=h, ts=ts):
                return wts.at[ts, pl.ds(1024 * h + quarter * origin + lo, size), :]

            mine = piece(me[h], 0, quarter)
            a = rcopy(mine, mine, sems[0], right[h])
            b = rcopy(mine, mine, sems[1], left[h])
            a.start()
            b.start()
            ring.append((k, h, a, b, sems, piece))
        if k == 0:
            cp_pw.wait_recv()
            proj(pj, to_ref(pp))
            cp_pp = rcopy(pp, r_pp, new_sem(), partner)
            cp_pp.start()
            for n in range(16):
                cols = slice(128 * n, 128 * n + 128)
                hid_t[cols, :] = hid[:, cols].T

    far = {0: [], 1: []}
    for k, h, a, b, sems, piece in ring:
        half = quarter // 2
        a.wait_recv()
        first = piece((me[h] + 3) % 4, 0, half)
        fa = rcopy(first, first, sems[2], right[h])
        fa.start()
        b.wait_recv()
        second = piece((me[h] + 1) % 4, half, half)
        fb = rcopy(second, second, sems[3], left[h])
        fb.start()
        far[k] += [fa, fb]

    for cp in far[0]:
        cp.wait_recv()
    proj(tp, to_ref(pf))
    cp_pf = rcopy(pf, r_pf, new_sem(), partner)
    cp_pf.start()
    for cp in far[1]:
        cp.wait_recv()
    proj(tf, to_ref(ff))
    cp_pf.wait_recv()
    z_sem = new_sem(NB)

    def block_z(b):
        rows = pl.ds(b * 128, 128)
        return rcopy(ff.at[rows, :], r_z.at[rows, :], z_sem + b, pair_same)

    @pl.loop(0, NB)
    def _(b):
        rows = pl.ds(b * 128, 128)
        ff[rows, :] = ff[rows, :] + r_pf[rows, :]
        block_z(b).start()

    cp_pp.wait_recv()
    cp_q.wait()
    cp_g.wait()
    live = live_ref[0]
    factor = HD ** -0.5
    kp_sem = new_sem(NB)
    kz_sem = new_sem(NB)
    kf_sem = new_sem(NB)

    def grad_copy(t, b, sem, to):
        ref = kvg.at[t, pl.ds(b * 128, 128), :]
        return rcopy(ref, ref, sem + b, to)

    @pl.loop(0, NB)
    def _(b):
        rows = pl.ds(b * 128, 128)
        block_z(b).wait_recv()
        kv = (own[rows, :] + r_pp[rows, :] + r_z[rows, :]).astype(BF16)
        key, val = kv[:, :HD], kv[:, HD:]
        qs = jnp.concatenate([qv[rows, HD * n:HD * n + HD] for n in range(NH)], axis=0)
        gs = jnp.concatenate([gv[rows, HD * n:HD * n + HD] for n in range(NH)], axis=0)
        start = jnp.broadcast_to(start_ref[pl.ds(b, 1), :], (128, 128)).T
        pos_u = lax.broadcasted_iota(jnp.int32, (128, 128), 1)
        pos_t = lax.broadcasted_iota(jnp.int32, (128, 128), 0)
        is_live = b < live
        lim = jnp.where(is_live, pos_t, -1)
        allowed = ((pos_u >= start) & (pos_u <= lim))[None]
        sc = (dot(qs, key, ((1,), (1,))) * factor).reshape(NH, 128, 128)
        top = jnp.max(jnp.where(allowed, sc, -1e30), axis=-1, keepdims=True)
        wt = jnp.where(allowed, jnp.exp(sc - top), 0.0)
        tot = jnp.sum(wt, axis=-1, keepdims=True)
        tot = jnp.where(is_live, tot, 1.0)
        prob = (wt * (1.0 / tot)).reshape(NH * 128, 128)
        low = prob.astype(BF16)
        att = dot(low, val, ((1,), (0,))).astype(BF16)
        rdot = jnp.sum(gs.astype(F32) * att.astype(F32), axis=-1, keepdims=True)
        pgrad = dot(gs, val, ((1,), (1,)))
        sg = (prob * (pgrad - rdot) * factor).astype(BF16)
        qgr = dot(sg, key, ((1,), (0,))).astype(BF16)
        for n in range(NH):
            qg[rows, HD * n:HD * n + HD] = qgr[128 * n:128 * n + 128, :]
        kvg[j, rows, :HD] = dot(sg, qs, ((0,), (0,))).astype(BF16)
        kvg[j, rows, HD:] = dot(low, gs, ((0,), (0,))).astype(BF16)
        grad_copy(j, b, kz_sem, pair_same).start()
        grad_copy(j, b, kp_sem, partner).start()

    cp_qo = pltpu.make_async_copy(qg, qg_out, new_loc())
    cp_qo.start()

    @pl.loop(0, NB)
    def _(b):
        grad_copy(tf, b, kz_sem, pair_same).wait_recv()
        grad_copy(tf, b, kf_sem, partner).start()

    @pl.loop(0, NB)
    def _(b):
        grad_copy(pj, b, kp_sem, partner).wait_recv()
        grad_copy(tp, b, kf_sem, partner).wait_recv()

    order = (0, 2, 1, 3)
    axis1 = {0: 0, 1: 0, 2: 1, 3: 1}

    def tiles(t, dest, lo, hi, store):
        sk, sd = (512, 128) if axis1[t] == 0 else (128, 512)

        @pl.loop(lo, hi)
        def _(k):
            row = pl.multiple_of(sk * k + sd * dest, 128)
            store(pl.ds(128 * k, 128), dot(hid_t[pl.ds(row, 128), :], kvg[t], ((1,), (0,))))

    def put(ref, t, low_=0):
        def store(rows, value):
            ref[t, rows, :] = value.astype(ref.dtype)
        return store

    p1 = {}

    def p1_far(t):
        h = axis1[t]
        tiles(t, (me[h] + 2) % 4, 0, 4, put(s_far, t))
        a = rcopy(s_far.at[t, 0:256, :], r_rel.at[t, 0:256, :], new_sem(), right[h])
        b = rcopy(s_far.at[t, 256:512, :], r_rel.at[t, 256:512, :], new_sem(), left[h])
        a.start()
        b.start()
        p1[t] = [a, b]

    def p1_direct(t):
        h = axis1[t]
        tiles(t, (me[h] + 1) % 4, 2, 4, put(s_rt, t))
        a = rcopy(s_rt.at[t, 256:512, :], r_nbl.at[t, 256:512, :], new_sem(), right[h])
        a.start()
        tiles(t, (me[h] + 3) % 4, 0, 2, put(s_lt, t))
        b = rcopy(s_lt.at[t, 0:256, :], r_nbr.at[t, 0:256, :], new_sem(), left[h])
        b.start()
        tiles(t, (me[h] + 1) % 4, 0, 2, put(st_rt, t))

        def low_rows(rows, value):
            st_lt[t, rows, :] = value

        tiles(t, (me[h] + 3) % 4, 2, 4, low_rows)
        tiles(t, me[h], 0, 4, put(acc, t))
        p1[t] += [a, b]

    def p1_relay(t):
        h = axis1[t]
        p1[t][0].wait_recv()
        s_rt[t, 0:256, :] = (st_rt[t, 0:256, :] + r_rel[t, 0:256, :].astype(F32)).astype(BF16)
        a = rcopy(s_rt.at[t, 0:256, :], r_nbl.at[t, 0:256, :], new_sem(), right[h])
        a.start()
        p1[t][1].wait_recv()
        s_lt[t, 256:512, :] = (st_lt[t, 256:512, :] + r_rel[t, 256:512, :].astype(F32)).astype(BF16)
        b = rcopy(s_lt.at[t, 256:512, :], r_nbr.at[t, 256:512, :], new_sem(), left[h])
        b.start()
        p1[t] += [a, b]

    p2 = {}

    def chunk(ref, t, k, lo, size):
        return ref.at[t, pl.ds(pl.multiple_of(128 * k + lo, 64), size), :]

    def p2_start(t):
        h = 1 - axis1[t]
        for cp in p1[t][2:]:
            cp.wait_recv()
        acc[t] = acc[t] + (r_nbl[t].astype(F32) + r_nbr[t].astype(F32))
        k2, kr, kl = (me[h] + 2) % 4, (me[h] + 1) % 4, (me[h] + 3) % 4
        cps = [
            rcopy(chunk(acc, t, k2, 0, 64), q_rel.at[t, 0:64, :], new_sem(), right[h]),
            rcopy(chunk(acc, t, k2, 64, 64), q_rel.at[t, 64:128, :], new_sem(), left[h]),
            rcopy(chunk(acc, t, kr, 64, 64), q_nbl.at[t, 64:128, :], new_sem(), right[h]),
            rcopy(chunk(acc, t, kl, 0, 64), q_nbr.at[t, 0:64, :], new_sem(), left[h]),
        ]
        for cp in cps:
            cp.start()
        p2[t] = cps

    def p2_relay(t):
        h = 1 - axis1[t]
        kr, kl = (me[h] + 1) % 4, (me[h] + 3) % 4
        p2[t][0].wait_recv()
        q_relay[t, 0:64, :] = chunk(acc, t, kr, 0, 64)[...] + q_rel[t, 0:64, :]
        a = rcopy(q_relay.at[t, 0:64, :], q_nbl.at[t, 0:64, :], new_sem(), right[h])
        a.start()
        p2[t][1].wait_recv()
        q_relay[t, 64:128, :] = chunk(acc, t, kl, 64, 64)[...] + q_rel[t, 64:128, :]
        b = rcopy(q_relay.at[t, 64:128, :], q_nbr.at[t, 64:128, :], new_sem(), left[h])
        b.start()
        p2[t] += [a, b]

    p3 = {}
    fin_sem = new_sem(4)
    fin_send = new_sem(4)

    def p3_start(t):
        h = 1 - axis1[t]
        for cp in p2[t][2:]:
            cp.wait_recv()
        z_acc[t] = chunk(acc, t, me[h], 0, 128)[...] + (q_nbl[t] + q_nbr[t])
        local = (zh == j) & (j == t)
        cp = pltpu.make_async_remote_copy(
            src_ref=z_acc.at[t], dst_ref=r_fin.at[zh],
            send_sem=snd.at[fin_send + t], recv_sem=rcv.at[fin_sem + zh],
            device_id=dev(j, y, x, t), device_id_type=MESH,
        )

        @pl.when(local)
        def _():
            r_fin[zh] = z_acc[t]

        @pl.when(jnp.logical_not(local))
        def _():
            cp.start()

        p3[t] = (local, cp)

    p1_far(0)
    p1_far(2)
    p1_direct(0)
    p1_direct(2)
    p1_far(1)
    p1_far(3)
    p1_relay(0)
    p1_relay(2)
    p1_direct(1)
    p1_direct(3)
    p1_relay(1)
    p1_relay(3)

    @pl.loop(0, KD // 256)
    def _(n):
        cols = pl.ds(pl.multiple_of(n * 256, 256), 256)
        total = jnp.zeros((ROWS, 256), F32)
        for t in range(4):
            part = dot(kvg[t], wts[t, cols, :], ((1,), (1,)))
            total = total + part.astype(BF16).astype(F32)
        hg[:, cols] = total.astype(BF16)

    cp_ho = pltpu.make_async_copy(hg, hg_out, new_loc())
    cp_ho.start()

    p2_start(0)
    p2_start(2)
    p2_relay(0)
    p2_relay(2)
    p2_start(1)
    p2_start(3)
    p3_start(0)
    p3_start(2)
    p2_relay(1)
    p2_relay(3)
    p3_start(1)
    p3_start(3)

    for k in range(4):
        @pl.when(jnp.logical_not((zh == j) & (zh == k)))
        def _():
            pltpu.make_async_remote_copy(
                src_ref=z_acc.at[k], dst_ref=r_fin.at[k],
                send_sem=snd.at[fin_send + k], recv_sem=rcv.at[fin_sem + k],
                device_id=dev(k, y, x, zh), device_id_type=MESH,
            ).wait_recv()

    out_v[...] = (r_fin[0] + r_fin[1]) + (r_fin[2] + r_fin[3])
    cp_wo = pltpu.make_async_copy(out_v, wg_out, new_loc())
    cp_wo.start()

    for cp in cp_z:
        cp.wait_send()
    for cp in (cp_pw, cp_pp, cp_pf):
        cp.wait_send()
    for k, h, a, b, sems, piece in ring:
        a.wait_send()
        b.wait_send()
    for cp in far[0] + far[1]:
        cp.wait_send()

    @pl.loop(0, NB)
    def _(b):
        block_z(b).wait_send()
        grad_copy(j, b, kz_sem, pair_same).wait_send()
        grad_copy(j, b, kp_sem, partner).wait_send()
        grad_copy(tf, b, kf_sem, partner).wait_send()

    for t in range(4):
        for cp in p1[t] + p2[t]:
            cp.wait_send()
        local, cp = p3[t]

        @pl.when(jnp.logical_not(local))
        def _():
            cp.wait_send()

    cp_qo.wait()
    cp_ho.wait()
    cp_wo.wait()


N_SEM = 160
N_LOC = 8


def on_device(hidden, kv_weight, queries, out_grad, live_blocks, doc_start):
    any_ = pl.BlockSpec(memory_space=pl.ANY)
    vm = pltpu.VMEM
    return pl.pallas_call(
        kernel,
        out_shape=(
            jax.ShapeDtypeStruct((ROWS, NH * HD), BF16),
            jax.ShapeDtypeStruct((ROWS, KD), BF16),
            jax.ShapeDtypeStruct((128, KC), F32),
        ),
        in_specs=[
            pl.BlockSpec(memory_space=pltpu.SMEM),
            pl.BlockSpec(memory_space=pltpu.VMEM),
            any_, any_, any_, any_,
        ],
        out_specs=(any_, any_, any_),
        scratch_shapes=[
            vm((ROWS, KD), BF16), vm((KD, ROWS), BF16), vm((4, KD, KC), BF16),
            vm((ROWS, NH * HD), BF16), vm((ROWS, NH * HD), BF16), vm((ROWS, NH * HD), BF16),
            vm((ROWS, KD), BF16),
            vm((ROWS, KC), F32), vm((ROWS, KC), F32), vm((ROWS, KC), F32), vm((ROWS, KC), F32),
            vm((ROWS, KC), F32), vm((ROWS, KC), F32), vm((ROWS, KC), F32),
            vm((4, ROWS, KC), BF16),
            vm((4, ROWS, KC), BF16), vm((4, ROWS, KC), BF16), vm((4, ROWS, KC), BF16),
            vm((4, ROWS, KC), F32), vm((4, ROWS, KC), F32), vm((4, ROWS, KC), F32),
            vm((4, ROWS, KC), BF16), vm((4, ROWS, KC), BF16), vm((4, ROWS, KC), BF16),
            vm((8, 128), F32),
            vm((4, 128, KC), F32), vm((4, 128, KC), F32), vm((4, 128, KC), F32), vm((4, 128, KC), F32),
            vm((4, 128, KC), F32), vm((4, 128, KC), F32), vm((128, KC), F32),
            pltpu.SemaphoreType.DMA((N_LOC,)),
            pltpu.SemaphoreType.DMA((N_SEM,)),
            pltpu.SemaphoreType.DMA((N_SEM,)),
        ],
        compiler_params=pltpu.CompilerParams(
            collective_id=0, has_side_effects=True, vmem_limit_bytes=60 * 1024 * 1024
        ),
        name="fused_step",
    )(live_blocks, doc_start.reshape(NB, 128), hidden, kv_weight, queries, out_grad)


def solution(mesh):
    in_specs = (
        P("dp", "tensor"),
        P(None, "tensor"),
        P("dp", "tensor"),
        P("dp", "tensor"),
        P("dp"),
        P("dp"),
    )
    out_specs = (P("dp", "tensor"), P("dp", "tensor"), P("dp", "tensor"))
    return jax.shard_map(
        on_device, mesh=mesh, in_specs=in_specs, out_specs=out_specs, check_vma=False
    )
```

time: 615 us -> 99.5 us (0.16)
  waiting for transfers between devices: 560 us -> 0 us
  Pallas kernels: 0 us -> 93.5 us
  matrix products: 25.1 us -> 0 us
  between operations: 14.6 us -> 1.3 us
  local copies, waits for them, and re-layouts: 13.5 us -> 4.39 us
    reduce_scatter x2 -> x0, waiting for transfers between devices: 475 us -> none  [the longest x1 353 us: on_device(): lax.psum_scatter(lax.dot_general(gathered, kv_grad, (((0,), (0,)), ((), (...]
    pallas_call x0 -> x1, Pallas kernels: none -> 93.5 us  [on_device(): pl.pallas_call(kernel, out_shape=(jax.ShapeDtypeStruct((ROWS, NH * HD), B...]
    all_gather x1 -> x0, waiting for transfers between devices: 83.8 us -> none  [on_device(): gathered = lax.all_gather(hidden, 'tensor', axis=1, tiled=True)]
    dot_general x9 -> x0, matrix products: 25.1 us -> none  [the longest x1 7.8 us: on_device(): lax.dot_general(kv_grad, kv_weight, (((1,), (1,)), ((), ())), preferred_e...]
  transfers between devices with their start and end apart: 3 -> 0, of which waited for: 3 -> 0; matrix products, arithmetic and copies ran while one was open for 3% -> 0% of each run, Pallas kernels for 0% -> 0%
where the time goes in v1:
time: 99.5 us; the launch traced here: 99.2 us
  Pallas kernels  93.5 us (94%)
  local copies, waits for them, and re-layouts  4.39 us (4%)
  between operations  1.3 us (1%)
    pallas_call x1, Pallas kernels, on_device(): pl.pallas_call(kernel, out_shape=(jax.ShapeDtypeStruct((ROWS, NH * HD), B...  93.5 us
    unnamed x7, local copies, waits for them, and re-layouts  4.39 us

profile of v1, /device:TPU:1, one launch (start us, length us, event | category | flops | bytes accessed | tf_op | source)
XLA Modules:
  0.0 99.2 jit_solution(194079121685282773)
XLA Ops:
  1.3 93.5 %fused_step.1 = (bf16[512,1024]{1,0:T(8,128)(2,1)}, bf16[512,2048]{1,0:T(8,128)(2,1)}, f32[128,256]{1,0:T(8,128)}) custom-call(s32[1]{0:T(128)S(6)} %copy.12.live_ref, s32[4,128]{1,0:T(4,128)} %bitcast.1, bf16[512,2048]{1,0:T(8,128)(2,1)} %hid_hbm.1, bf16[8192,256]{1,0:T(8,128)(2,1)} %w_hbm.1, bf16[512,1024]{1,0:T(8,128)(2,1)} %q_hbm.1, bf16[512,1024]{1,0:T(8,128)(2,1)} %g_hbm.1), custom_call_target="tpu_custom_call" | custom-call | tf_op jit(solution)/shard_map/fused_step/pallas_call | solution.py:457
  94.8 0.0 copy-start
  94.8 2.4 %copy.13 = bf16[512,1024]{1,0:T(8,128)(2,1)} copy(bf16[512,1024]{1,0:T(8,128)(2,1)} %get-tuple-element.6) | data formatting | bytes 2097152
  97.2 0.0 copy-done
  97.2 0.0 copy-start.1
  97.2 1.3 %copy.14 = bf16[512,2048]{1,0:T(8,128)(2,1)} copy(bf16[512,2048]{1,0:T(8,128)(2,1)S(1)} %copy-done) | data formatting | bytes 4194304
  98.6 0.0 copy-done.1
  98.6 0.7 copy.15
Async XLA Ops:
  94.8 2.4 %copy-start = (bf16[512,2048]{1,0:T(8,128)(2,1)S(1)}, bf16[512,2048]{1,0:T(8,128)(2,1)}, u32[]{:S(2)}) copy-start(bf16[512,2048]{1,0:T(8,128)(2,1)} %get-tuple-element.7) | copy-start | bytes 6291460
  97.2 1.3 %copy-start.1 = (f32[128,256]{1,0:T(8,128)S(1)}, f32[128,256]{1,0:T(8,128)}, u32[]{:S(2)}) copy-start(f32[128,256]{1,0:T(8,128)} %get-tuple-element.8) | copy-start | bytes 393220

commit v2 on v1

v2 whole, which is shorter than its diff:
```python
import jax
import jax.numpy as jnp
from jax import lax
from jax.experimental import pallas as pl
from jax.experimental.pallas import tpu as pltpu
from jax.sharding import PartitionSpec as P

BF16 = jnp.bfloat16
F32 = jnp.float32
HD = 128
ROWS = 512
NB = 4
NH = 8
KD = 2048
KC = 256
MESH = pl.DeviceIdType.MESH


def dot(a, b, dims):
    return lax.dot_general(a, b, (dims, ((), ())), preferred_element_type=F32)


def kernel(
    live_ref, start_ref, hid_hbm, w_hbm, q_hbm, g_hbm,
    qg, hg, wg_out,
    hid, hid_t, wts, qv, gv,
    own, pp, pf, ff, r_pp, r_pf, r_z, kvg,
    s_far, s_rt, s_lt, st_rt, st_lt, acc, r_rel, r_nbl, r_nbr,
    q_relay, q_rel, q_nbl, q_nbr,
    z_acc, r_fin,
    loc, snd, rcv,
):
    counter = [0, 0]

    def new_sem(count=1):
        first = counter[0]
        counter[0] += count
        return first

    def new_loc():
        counter[1] += 1
        return loc.at[counter[1] - 1]

    dp = lax.axis_index("dp")
    j = lax.axis_index("tensor")
    zh = dp // 16
    y = (dp // 4) % 4
    x = dp % 4
    zl = j // 2
    c = j % 2
    pj = 2 * zl + 1 - c
    fz = 2 * (1 - zl)
    tf = fz + c
    tp = fz + 1 - c

    def dev(zh_, y_, x_, t_):
        return {"dp": zh_ * 16 + y_ * 4 + x_, "tensor": t_}

    partner = dev(zh, y, x, pj)
    pair_same = dev(zh, y, x, tf)
    pair_other = dev(zh, y, x, tp)
    zo = (zh + 2 * zl + 3) % 4
    oth_same = dev(zo, y, x, tf)
    oth_other = dev(zo, y, x, tp)
    right = (dev(zh, y, (x + 1) % 4, j), dev(zh, (y + 1) % 4, x, j))
    left = (dev(zh, y, (x + 3) % 4, j), dev(zh, (y + 3) % 4, x, j))
    me = (x, y)

    sent = []

    def finish():
        for wait in sent:
            wait()

    def rcopy(src, dst, sem, to, keep=True):
        cp = pltpu.make_async_remote_copy(
            src_ref=src, dst_ref=dst, send_sem=snd.at[sem], recv_sem=rcv.at[sem],
            device_id=to, device_id_type=MESH,
        )
        if keep:
            sent.append(cp.wait_send)
        return cp

    def looped(make):
        def wait():
            @pl.loop(0, NB)
            def _(b):
                make(b).wait_send()

        sent.append(wait)

    cp_own = pltpu.make_async_copy(w_hbm.at[pl.ds(KD * j, KD), :], wts.at[j], new_loc())
    cp_own.start()
    cp_hid = pltpu.make_async_copy(hid_hbm, hid, new_loc())
    cp_hid.start()

    barrier = pltpu.get_barrier_semaphore()

    def greet(to):
        pl.semaphore_signal(barrier, inc=1, device_id=to, device_id_type=MESH)

    for to in (partner, pair_same, pair_other, oth_same, oth_other) + right + left:
        greet(to)
    for k in range(4):
        @pl.when(jnp.logical_not((zh == j) & (j == k)))
        def _():
            greet(dev(j, y, x, k))

        @pl.when(jnp.logical_not((zh == j) & (zh == k)))
        def _():
            greet(dev(k, y, x, zh))
    own_case = jnp.where(zh == j, 1, 0)
    pl.semaphore_wait(barrier, 17 - 2 * own_case)

    quarter = KD // 8
    piece_rows = quarter // 2
    cp_z = {}
    for k in range(2):
        cd = (1 - c) if k == 0 else c
        td = fz + cd
        for n in range(2):
            for h in range(2):
                to = ((pair_other, pair_same), (oth_other, oth_same))[h][k]
                off = 1024 * h + quarter * me[h] + piece_rows * n
                cp = rcopy(
                    w_hbm.at[pl.ds(KD * td + off, piece_rows), :],
                    wts.at[j, pl.ds(off, piece_rows), :], new_sem(), to,
                )
                cp.start()
                cp_z[k, n, h] = cp
    cp_pw = rcopy(w_hbm.at[pl.ds(KD * pj, KD), :], wts.at[j], new_sem(), partner)
    cp_pw.start()
    cp_q = pltpu.make_async_copy(q_hbm, qv, new_loc())
    cp_q.start()
    cp_g = pltpu.make_async_copy(g_hbm, gv, new_loc())
    cp_g.start()

    def proj(t, store):
        @pl.loop(0, 2)
        def _(n):
            rows = pl.ds(n * 256, 256)
            store(rows, dot(hid[rows, :], wts[t], ((1,), (0,))))

    def to_ref(ref):
        def store(rows, value):
            ref[rows, :] = value
        return store

    ring = {}

    def ring_near(k):
        ts = (tp, tf)[k]
        for n in range(2):
            for h in range(2):
                cp_z[k, n, h].wait_recv()
                sems = [new_sem() for _ in range(4)]

                def piece(origin, lo, size, h=h, ts=ts, n=n):
                    off = 1024 * h + quarter * origin + piece_rows * n + lo
                    return wts.at[ts, pl.ds(off, size), :]

                mine = piece(me[h], 0, piece_rows)
                a = rcopy(mine, mine, sems[0], right[h])
                b = rcopy(mine, mine, sems[1], left[h])
                a.start()
                b.start()
                ring[k, n, h] = (a, b, sems, piece)

    far = {0: [], 1: []}

    def ring_far(k):
        half = piece_rows // 2
        for n in range(2):
            for h in range(2):
                a, b, sems, piece = ring[k, n, h]
                a.wait_recv()
                first = piece((me[h] + 3) % 4, 0, half)
                fa = rcopy(first, first, sems[2], right[h])
                fa.start()
                b.wait_recv()
                second = piece((me[h] + 1) % 4, half, half)
                fb = rcopy(second, second, sems[3], left[h])
                fb.start()
                far[k] += [fa, fb]

    ring_near(0)
    cp_hid.wait()
    cp_own.wait()
    proj(j, to_ref(own))
    ring_near(1)
    ring_far(0)
    cp_pw.wait_recv()
    proj(pj, to_ref(pp))
    cp_pp = rcopy(pp, r_pp, new_sem(), partner)
    cp_pp.start()
    ring_far(1)

    for cp in far[0]:
        cp.wait_recv()
    proj(tp, to_ref(pf))
    cp_pf = rcopy(pf, r_pf, new_sem(), partner)
    cp_pf.start()
    for cp in far[1]:
        cp.wait_recv()
    proj(tf, to_ref(ff))
    cp_pf.wait_recv()
    z_sem = new_sem(NB)

    def block_z(b):
        rows = pl.ds(b * 128, 128)
        return rcopy(ff.at[rows, :], r_z.at[rows, :], z_sem + b, pair_same, keep=False)

    @pl.loop(0, NB)
    def _(b):
        rows = pl.ds(b * 128, 128)
        ff[rows, :] = ff[rows, :] + r_pf[rows, :]
        block_z(b).start()

    looped(block_z)
    cp_pp.wait_recv()
    cp_q.wait()
    cp_g.wait()
    live = live_ref[0]
    factor = HD ** -0.5
    kp_sem = new_sem(NB)
    kz_sem = new_sem(NB)
    kf_sem = new_sem(NB)

    def grad_copy(t, b, sem, to):
        ref = kvg.at[t, pl.ds(b * 128, 128), :]
        return rcopy(ref, ref, sem + b, to, keep=False)

    @pl.loop(0, NB)
    def _(b):
        rows = pl.ds(b * 128, 128)
        for n in range(4):
            cols = pl.ds(pl.multiple_of(512 * b + 128 * n, 128), 128)
            hid_t[cols, :] = hid[:, cols].T
        block_z(b).wait_recv()
        kv = (own[rows, :] + r_pp[rows, :] + r_z[rows, :]).astype(BF16)
        key, val = kv[:, :HD], kv[:, HD:]
        qs = jnp.concatenate([qv[rows, HD * n:HD * n + HD] for n in range(NH)], axis=0)
        gs = jnp.concatenate([gv[rows, HD * n:HD * n + HD] for n in range(NH)], axis=0)
        start = jnp.broadcast_to(start_ref[pl.ds(b, 1), :], (128, 128)).T
        pos_u = lax.broadcasted_iota(jnp.int32, (128, 128), 1)
        pos_t = lax.broadcasted_iota(jnp.int32, (128, 128), 0)
        is_live = b < live
        lim = jnp.where(is_live, pos_t, -1)
        allowed = ((pos_u >= start) & (pos_u <= lim))[None]
        sc = (dot(qs, key, ((1,), (1,))) * factor).reshape(NH, 128, 128)
        top = jnp.max(jnp.where(allowed, sc, -1e30), axis=-1, keepdims=True)
        wt = jnp.where(allowed, jnp.exp(sc - top), 0.0)
        tot = jnp.sum(wt, axis=-1, keepdims=True)
        tot = jnp.where(is_live, tot, 1.0)
        prob = (wt * (1.0 / tot)).reshape(NH * 128, 128)
        low = prob.astype(BF16)
        att = dot(low, val, ((1,), (0,))).astype(BF16)
        rdot = jnp.sum(gs.astype(F32) * att.astype(F32), axis=-1, keepdims=True)
        pgrad = dot(gs, val, ((1,), (1,)))
        sg = (prob * (pgrad - rdot) * factor).astype(BF16)
        qgr = dot(sg, key, ((1,), (0,))).astype(BF16)
        for n in range(NH):
            qg[rows, HD * n:HD * n + HD] = qgr[128 * n:128 * n + 128, :]
        kvg[j, rows, :HD] = dot(sg, qs, ((0,), (0,))).astype(BF16)
        kvg[j, rows, HD:] = dot(low, gs, ((0,), (0,))).astype(BF16)
        grad_copy(j, b, kz_sem, pair_same).start()
        grad_copy(j, b, kp_sem, partner).start()

    looped(lambda b: grad_copy(j, b, kz_sem, pair_same))
    looped(lambda b: grad_copy(j, b, kp_sem, partner))
    @pl.loop(0, NB)
    def _(b):
        grad_copy(tf, b, kz_sem, pair_same).wait_recv()
        grad_copy(tf, b, kf_sem, partner).start()

    looped(lambda b: grad_copy(tf, b, kf_sem, partner))

    @pl.loop(0, NB)
    def _(b):
        grad_copy(pj, b, kp_sem, partner).wait_recv()
        grad_copy(tp, b, kf_sem, partner).wait_recv()

    axis1 = (0, 0, 1, 1)
    jobs = ((0, 0), (2, 0), (0, 1), (2, 1), (1, 0), (3, 0), (1, 1), (3, 1))

    def partial(i, dest):
        t, s = jobs[i]
        sk, sd = (512, 128) if axis1[t] == 0 else (128, 512)
        lhs = [
            hid_t[pl.ds(pl.multiple_of(sk * k + sd * dest + 64 * s, 64), 64), :]
            for k in range(4)
        ]
        return dot(jnp.concatenate(lhs, axis=0), kvg[t], ((1,), (0,)))

    lo, hi = slice(0, 128), slice(128, 256)
    p1 = {}

    def p1_far(i):
        h = axis1[jobs[i][0]]
        s_far[i] = partial(i, (me[h] + 2) % 4).astype(BF16)
        a = rcopy(s_far.at[i, lo, :], r_rel.at[i, lo, :], new_sem(), right[h])
        b = rcopy(s_far.at[i, hi, :], r_rel.at[i, hi, :], new_sem(), left[h])
        a.start()
        b.start()
        p1[i] = [a, b]

    def p1_direct(i):
        h = axis1[jobs[i][0]]
        part = partial(i, (me[h] + 1) % 4)
        s_rt[i, hi, :] = part[hi, :].astype(BF16)
        st_rt[i] = part[lo, :]
        a = rcopy(s_rt.at[i, hi, :], r_nbl.at[i, hi, :], new_sem(), right[h])
        a.start()
        part = partial(i, (me[h] + 3) % 4)
        s_lt[i, lo, :] = part[lo, :].astype(BF16)
        st_lt[i] = part[hi, :]
        b = rcopy(s_lt.at[i, lo, :], r_nbr.at[i, lo, :], new_sem(), left[h])
        b.start()
        p1[i] += [a, b]

    def p1_own(i):
        acc[i] = partial(i, me[axis1[jobs[i][0]]])

    def p1_relay(i):
        h = axis1[jobs[i][0]]
        p1[i][0].wait_recv()
        s_rt[i, lo, :] = (st_rt[i] + r_rel[i, lo, :].astype(F32)).astype(BF16)
        a = rcopy(s_rt.at[i, lo, :], r_nbl.at[i, lo, :], new_sem(), right[h])
        a.start()
        p1[i][1].wait_recv()
        s_lt[i, hi, :] = (st_lt[i] + r_rel[i, hi, :].astype(F32)).astype(BF16)
        b = rcopy(s_lt.at[i, hi, :], r_nbr.at[i, hi, :], new_sem(), left[h])
        b.start()
        p1[i] += [a, b]

    p2 = {}

    def chunk(i, k, low, size):
        return acc.at[i, pl.ds(pl.multiple_of(64 * k + low, 32), size), :]

    def p2_start(i):
        h = 1 - axis1[jobs[i][0]]
        for cp in p1[i][2:]:
            cp.wait_recv()
        acc[i] = acc[i] + (r_nbl[i].astype(F32) + r_nbr[i].astype(F32))
        k2, kr, kl = (me[h] + 2) % 4, (me[h] + 1) % 4, (me[h] + 3) % 4
        cps = [
            rcopy(chunk(i, k2, 0, 32), q_rel.at[i, 0:32, :], new_sem(), right[h]),
            rcopy(chunk(i, k2, 32, 32), q_rel.at[i, 32:64, :], new_sem(), left[h]),
            rcopy(chunk(i, kr, 32, 32), q_nbl.at[i, 32:64, :], new_sem(), right[h]),
            rcopy(chunk(i, kl, 0, 32), q_nbr.at[i, 0:32, :], new_sem(), left[h]),
        ]
        for cp in cps:
            cp.start()
        p2[i] = cps

    def p2_relay(i):
        h = 1 - axis1[jobs[i][0]]
        kr, kl = (me[h] + 1) % 4, (me[h] + 3) % 4
        p2[i][0].wait_recv()
        q_relay[i, 0:32, :] = chunk(i, kr, 0, 32)[...] + q_rel[i, 0:32, :]
        a = rcopy(q_relay.at[i, 0:32, :], q_nbl.at[i, 0:32, :], new_sem(), right[h])
        a.start()
        p2[i][1].wait_recv()
        q_relay[i, 32:64, :] = chunk(i, kl, 32, 32)[...] + q_rel[i, 32:64, :]
        b = rcopy(q_relay.at[i, 32:64, :], q_nbr.at[i, 32:64, :], new_sem(), left[h])
        b.start()
        p2[i] += [a, b]

    fin_send = new_sem(8)
    fin_recv = new_sem(8)

    def fin_copy(t, s, source, to):
        rows = pl.ds(64 * s, 64)
        return pltpu.make_async_remote_copy(
            src_ref=z_acc.at[t, rows, :], dst_ref=r_fin.at[source, rows, :],
            send_sem=snd.at[fin_send + 2 * t + s], recv_sem=rcv.at[fin_recv + 2 * source + s],
            device_id=to, device_id_type=MESH,
        )

    def p3_start(i):
        t, s = jobs[i]
        h = 1 - axis1[t]
        for cp in p2[i][2:]:
            cp.wait_recv()
        rows = pl.ds(64 * s, 64)
        z_acc[t, rows, :] = chunk(i, me[h], 0, 64)[...] + (q_nbl[i] + q_nbr[i])
        local = (zh == j) & (j == t)
        cp = fin_copy(t, s, zh, dev(j, y, x, t))

        @pl.when(local)
        def _():
            r_fin[zh, rows, :] = z_acc[t, rows, :]

        @pl.when(jnp.logical_not(local))
        def _():
            cp.start()

        @sent.append
        def _():
            @pl.when(jnp.logical_not(local))
            def _():
                cp.wait_send()

    def both(f, n):
        f(2 * n)
        f(2 * n + 1)

    def hidden_grad(first, last):
        @pl.loop(first, last)
        def _(n):
            cols = pl.ds(pl.multiple_of(n * 256, 256), 256)
            total = jnp.zeros((ROWS, 256), F32)
            for t in range(4):
                part = dot(kvg[t], wts[t, cols, :], ((1,), (1,)))
                total = total + part.astype(BF16).astype(F32)
            hg[:, cols] = total.astype(BF16)

    both(p1_far, 0)
    both(p1_direct, 0)
    both(p1_far, 1)
    both(p1_own, 0)
    both(p1_relay, 0)
    both(p1_direct, 1)
    both(p1_far, 2)
    both(p1_own, 1)
    both(p1_relay, 1)
    both(p1_direct, 2)
    both(p2_start, 0)
    both(p1_far, 3)
    both(p1_relay, 2)
    both(p2_relay, 0)
    both(p1_direct, 3)
    both(p1_own, 2)
    both(p1_own, 3)
    both(p2_start, 1)
    both(p3_start, 0)
    both(p1_relay, 3)
    both(p2_relay, 1)
    hidden_grad(0, 3)
    both(p2_start, 2)
    both(p3_start, 1)
    both(p2_relay, 2)
    hidden_grad(3, 6)
    both(p2_start, 3)
    both(p3_start, 2)
    both(p2_relay, 3)
    hidden_grad(6, 8)
    both(p3_start, 3)
    for k in range(4):
        @pl.when(jnp.logical_not((zh == j) & (zh == k)))
        def _():
            for s in range(2):
                fin_copy(k, s, k, dev(k, y, x, zh)).wait_recv()

    wg_out[...] = (r_fin[0] + r_fin[1]) + (r_fin[2] + r_fin[3])
    finish()


N_SEM = 192
N_LOC = 8


def leave(qg, hg, wg, qg_out, hg_out, wg_out, sems):
    cps = [
        pltpu.make_async_copy(src, dst, sems.at[n])
        for n, (src, dst) in enumerate(((hg, hg_out), (qg, qg_out), (wg, wg_out)))
    ]
    for cp in cps:
        cp.start()
    for cp in cps:
        cp.wait()


def on_device(hidden, kv_weight, queries, out_grad, live_blocks, doc_start):
    any_ = pl.BlockSpec(memory_space=pl.ANY)
    vmem = pl.BlockSpec(memory_space=pltpu.VMEM)
    vm = pltpu.VMEM
    results = ((ROWS, NH * HD), BF16), ((ROWS, KD), BF16), ((128, KC), F32)
    fused = pl.pallas_call(
        kernel,
        out_shape=tuple(vm(*r) for r in results),
        in_specs=[pl.BlockSpec(memory_space=pltpu.SMEM), vmem, any_, any_, any_, any_],
        out_specs=(vmem, vmem, vmem),
        scratch_shapes=[
            vm((ROWS, KD), BF16), vm((KD, ROWS), BF16), vm((4, KD, KC), BF16),
            vm((ROWS, NH * HD), BF16), vm((ROWS, NH * HD), BF16),
            vm((ROWS, KC), F32), vm((ROWS, KC), F32), vm((ROWS, KC), F32), vm((ROWS, KC), F32),
            vm((ROWS, KC), F32), vm((ROWS, KC), F32), vm((ROWS, KC), F32),
            vm((4, ROWS, KC), BF16),
            vm((8, 256, KC), BF16), vm((8, 256, KC), BF16), vm((8, 256, KC), BF16),
            vm((8, 128, KC), F32), vm((8, 128, KC), F32), vm((8, 256, KC), F32),
            vm((8, 256, KC), BF16), vm((8, 256, KC), BF16), vm((8, 256, KC), BF16),
            vm((8, 64, KC), F32), vm((8, 64, KC), F32), vm((8, 64, KC), F32), vm((8, 64, KC), F32),
            vm((4, 128, KC), F32), vm((4, 128, KC), F32),
            pltpu.SemaphoreType.DMA((N_LOC,)),
            pltpu.SemaphoreType.DMA((N_SEM,)),
            pltpu.SemaphoreType.DMA((N_SEM,)),
        ],
        compiler_params=pltpu.CompilerParams(
            collective_id=0, has_side_effects=True, vmem_limit_bytes=58 * 1024 * 1024
        ),
        name="fused_step",
    )(live_blocks, doc_start.reshape(NB, 128), hidden, kv_weight, queries, out_grad)
    return pl.pallas_call(
        leave,
        out_shape=tuple(jax.ShapeDtypeStruct(*r) for r in results),
        in_specs=[vmem, vmem, vmem],
        out_specs=(any_, any_, any_),
        scratch_shapes=[pltpu.SemaphoreType.DMA((3,))],
        compiler_params=pltpu.CompilerParams(vmem_limit_bytes=1024 * 1024),
        name="leave",
    )(*fused)


def solution(mesh):
    in_specs = (
        P("dp", "tensor"),
        P(None, "tensor"),
        P("dp", "tensor"),
        P("dp", "tensor"),
        P("dp"),
        P("dp"),
    )
    out_specs = (P("dp", "tensor"), P("dp", "tensor"), P("dp", "tensor"))
    return jax.shard_map(
        on_device, mesh=mesh, in_specs=in_specs, out_specs=out_specs, check_vma=False
    )
```

time: 99.5 us -> 94.2 us (0.947)
  local copies, waits for them, and re-layouts: 4.39 us -> 0 us
    unnamed x7 -> x0, local copies, waits for them, and re-layouts: 4.39 us -> none
    pallas_call x1 -> x2, Pallas kernels: 93.5 us -> 92.8 us  [the longest x1 91.1 us: on_device(): pl.pallas_call(kernel, out_shape=tuple((vm(*r) for r in results)), in_spe...]
where the time goes in v2:
time: 94.2 us; the launch traced here: 94.1 us
  Pallas kernels  92.8 us (99%)
  between operations  1.29 us (1%)
    pallas_call x1, Pallas kernels, on_device(): pl.pallas_call(kernel, out_shape=tuple((vm(*r) for r in results)), in_spe...  91.1 us

profile of v2, /device:TPU:1, one launch (start us, length us, event | category | flops | bytes accessed | tf_op | source)
XLA Modules:
  0.0 94.1 jit_solution(9962531368459529017)
XLA Ops:
  1.3 91.1 %fused_step.1 = (bf16[512,1024]{1,0:T(8,128)(2,1)S(1)}, bf16[512,2048]{1,0:T(8,128)(2,1)S(1)}, f32[128,256]{1,0:T(8,128)S(1)}) custom-call(s32[1]{0:T(128)S(6)} %copy.9.live_ref, s32[4,128]{1,0:T(4,128)} %bitcast.1, bf16[512,2048]{1,0:T(8,128)(2,1)} %hid_hbm.1, bf16[8192,256]{1,0:T(8,128)(2,1)} %w_hbm.1, bf16[512,1024]{1,0:T(8,128)(2,1)} %q_hbm.1, ...), custom_call_target="tpu_custom_call" | custom-call | tf_op jit(solution)/shard_map/fused_step/pallas_call | solution.py:480
  92.4 1.7 %leave.1 = (bf16[512,1024]{1,0:T(8,128)(2,1)}, bf16[512,2048]{1,0:T(8,128)(2,1)}, f32[128,256]{1,0:T(8,128)}) custom-call(bf16[512,1024]{1,0:T(8,128)(2,1)S(1)} %get-tuple-element.6.qg, bf16[512,2048]{1,0:T(8,128)(2,1)S(1)} %get-tuple-element.7.hg, f32[128,256]{1,0:T(8,128)S(1)} %get-tuple-element.8.wg), custom_call_target="tpu_custom_call" | custom-call | tf_op jit(solution)/shard_map/leave/pallas_call | solution.py:505

commit v3 on v2

--- a/solution.py
+++ b/solution.py
@@ -25,8 +25,7 @@
     qg, hg, wg_out,
     hid, hid_t, wts, qv, gv,
     own, pp, pf, ff, r_pp, r_pf, r_z, kvg,
-    s_far, s_rt, s_lt, st_rt, st_lt, acc, r_rel, r_nbl, r_nbr,
-    q_relay, q_rel, q_nbl, q_nbr,
+    hx, kx, acc, s_far, s_rt, s_lt, q_far, q_nbl, q_nbr,
     z_acc, r_fin,
     loc, snd, rcv,
 ):
@@ -64,6 +63,7 @@
     oth_other = dev(zo, y, x, tp)
     right = (dev(zh, y, (x + 1) % 4, j), dev(zh, (y + 1) % 4, x, j))
     left = (dev(zh, y, (x + 3) % 4, j), dev(zh, (y + 3) % 4, x, j))
+    across = (dev(zh, y, (x + 2) % 4, j), dev(zh, (y + 2) % 4, x, j))
     me = (x, y)
 
     sent = []
@@ -99,7 +99,7 @@
     def greet(to):
         pl.semaphore_signal(barrier, inc=1, device_id=to, device_id_type=MESH)
 
-    for to in (partner, pair_same, pair_other, oth_same, oth_other) + right + left:
+    for to in (partner, pair_same, pair_other, oth_same, oth_other) + right + left + across:
         greet(to)
     for k in range(4):
         @pl.when(jnp.logical_not((zh == j) & (j == k)))
@@ -110,7 +110,7 @@
         def _():
             greet(dev(k, y, x, zh))
     own_case = jnp.where(zh == j, 1, 0)
-    pl.semaphore_wait(barrier, 17 - 2 * own_case)
+    pl.semaphore_wait(barrier, 19 - 2 * own_case)
 
     quarter = KD // 8
     piece_rows = quarter // 2
@@ -183,8 +183,37 @@
                 fb.start()
                 far[k] += [fa, fb]
 
+    cp_hid.wait()
+
+    @pl.loop(0, 4)
+    def _(k):
+        for n in range(4):
+            cols = pl.ds(pl.multiple_of(512 * k + 128 * n, 128), 128)
+            hid_t[k, n] = hid[:, cols].T
+
+    def block_rows(h, step):
+        dest = (me[h] + step) % 4
+        return hid_t.at[:, dest] if h == 0 else hid_t.at[dest]
+
+    h_near, h_far = [], []
+
+    def send_hidden(first, size):
+        for h in range(2):
+            for slot, step, to in ((0, 1, right[h]), (1, 3, left[h])):
+                part = pl.ds(first, size)
+                cp = rcopy(block_rows(h, step).at[part], hx.at[h, slot, part], new_sem(), to)
+                cp.start()
+                h_near.append(cp)
+
+    def send_hidden_rest():
+        send_hidden(2, 2)
+        for h in range(2):
+            cp = rcopy(block_rows(h, 2), hx.at[h, 2], new_sem(), across[h])
+            cp.start()
+            h_far.append(cp)
+
+    send_hidden(0, 2)
     ring_near(0)
-    cp_hid.wait()
     cp_own.wait()
     proj(j, to_ref(own))
     ring_near(1)
@@ -193,7 +222,9 @@
     proj(pj, to_ref(pp))
     cp_pp = rcopy(pp, r_pp, new_sem(), partner)
     cp_pp.start()
+
     ring_far(1)
+    send_hidden_rest()
 
     for cp in far[0]:
         cp.wait_recv()
@@ -230,12 +261,50 @@
         ref = kvg.at[t, pl.ds(b * 128, 128), :]
         return rcopy(ref, ref, sem + b, to, keep=False)
 
+    near_sem = [[new_sem(NB), new_sem(NB)] for _ in range(2)]
+    far_sem = [new_sem(NB) for _ in range(2)]
+    share_sem = [[new_sem(NB) for _ in range(3)] for _ in range(2)]
+    group = (j, tf)
+
+    def near(h, slot, b):
+        rows = pl.ds(b * 128, 128)
+        return rcopy(
+            kvg.at[group[h], rows, :], kx.at[h, slot, c, rows, :], near_sem[h][slot] + b,
+            (right, left)[slot][h], keep=False,
+        )
+
+    def far_on(h, b):
+        rows = pl.ds(b * 128, 128)
+        return rcopy(
+            kvg.at[group[h], rows, :], kx.at[h, 2, c, rows, :], far_sem[h] + b,
+            across[h], keep=False,
+        )
+
+    def spread(h, b):
+        near(h, 0, b).start()
+        near(h, 1, b).start()
+        far_on(h, b).start()
+
+    def share(h, slot, b, g):
+        ref = kx.at[h, slot, g, pl.ds(b * 128, 128), :]
+        return rcopy(ref, ref, share_sem[h][slot] + b, partner, keep=False)
+
+    def collect(h, b):
+        near(h, 0, b).wait_recv()
+        share(h, 0, b, c).start()
+        near(h, 1, b).wait_recv()
+        share(h, 1, b, c).start()
+        far_on(h, b).wait_recv()
+        share(h, 2, b, c).start()
+
+    def pass_z(b):
+        grad_copy(tf, b, kz_sem, pair_same).wait_recv()
+        spread(1, b)
+        grad_copy(tf, b, kf_sem, partner).start()
+
     @pl.loop(0, NB)
     def _(b):
         rows = pl.ds(b * 128, 128)
-        for n in range(4):
-            cols = pl.ds(pl.multiple_of(512 * b + 128 * n, 128), 128)
-            hid_t[cols, :] = hid[:, cols].T
         block_z(b).wait_recv()
         kv = (own[rows, :] + r_pp[rows, :] + r_z[rows, :]).astype(BF16)
         key, val = kv[:, :HD], kv[:, HD:]
@@ -264,133 +333,100 @@
         kvg[j, rows, :HD] = dot(sg, qs, ((0,), (0,))).astype(BF16)
         kvg[j, rows, HD:] = dot(low, gs, ((0,), (0,))).astype(BF16)
         grad_copy(j, b, kz_sem, pair_same).start()
+        spread(0, b)
         grad_copy(j, b, kp_sem, partner).start()
+
+        @pl.when(b >= 1)
+        def _():
+            pass_z(b - 1)
+            collect(0, b - 1)
 
     looped(lambda b: grad_copy(j, b, kz_sem, pair_same))
     looped(lambda b: grad_copy(j, b, kp_sem, partner))
-    @pl.loop(0, NB)
-    def _(b):
-        grad_copy(tf, b, kz_sem, pair_same).wait_recv()
-        grad_copy(tf, b, kf_sem, partner).start()
-
     looped(lambda b: grad_copy(tf, b, kf_sem, partner))
-
-    @pl.loop(0, NB)
-    def _(b):
-        grad_copy(pj, b, kp_sem, partner).wait_recv()
-        grad_copy(tp, b, kf_sem, partner).wait_recv()
-
-    axis1 = (0, 0, 1, 1)
-    jobs = ((0, 0), (2, 0), (0, 1), (2, 1), (1, 0), (3, 0), (1, 1), (3, 1))
-
-    def partial(i, dest):
-        t, s = jobs[i]
-        sk, sd = (512, 128) if axis1[t] == 0 else (128, 512)
-        lhs = [
-            hid_t[pl.ds(pl.multiple_of(sk * k + sd * dest + 64 * s, 64), 64), :]
-            for k in range(4)
-        ]
-        return dot(jnp.concatenate(lhs, axis=0), kvg[t], ((1,), (0,)))
-
-    lo, hi = slice(0, 128), slice(128, 256)
-    p1 = {}
-
-    def p1_far(i):
-        h = axis1[jobs[i][0]]
-        s_far[i] = partial(i, (me[h] + 2) % 4).astype(BF16)
-        a = rcopy(s_far.at[i, lo, :], r_rel.at[i, lo, :], new_sem(), right[h])
-        b = rcopy(s_far.at[i, hi, :], r_rel.at[i, hi, :], new_sem(), left[h])
-        a.start()
-        b.start()
-        p1[i] = [a, b]
-
-    def p1_direct(i):
-        h = axis1[jobs[i][0]]
-        part = partial(i, (me[h] + 1) % 4)
-        s_rt[i, hi, :] = part[hi, :].astype(BF16)
-        st_rt[i] = part[lo, :]
-        a = rcopy(s_rt.at[i, hi, :], r_nbl.at[i, hi, :], new_sem(), right[h])
-        a.start()
-        part = partial(i, (me[h] + 3) % 4)
-        s_lt[i, lo, :] = part[lo, :].astype(BF16)
-        st_lt[i] = part[hi, :]
-        b = rcopy(s_lt.at[i, lo, :], r_nbr.at[i, lo, :], new_sem(), left[h])
-        b.start()
-        p1[i] += [a, b]
-
-    def p1_own(i):
-        acc[i] = partial(i, me[axis1[jobs[i][0]]])
-
-    def p1_relay(i):
-        h = axis1[jobs[i][0]]
-        p1[i][0].wait_recv()
-        s_rt[i, lo, :] = (st_rt[i] + r_rel[i, lo, :].astype(F32)).astype(BF16)
-        a = rcopy(s_rt.at[i, lo, :], r_nbl.at[i, lo, :], new_sem(), right[h])
-        a.start()
-        p1[i][1].wait_recv()
-        s_lt[i, hi, :] = (st_lt[i] + r_rel[i, hi, :].astype(F32)).astype(BF16)
-        b = rcopy(s_lt.at[i, hi, :], r_nbr.at[i, hi, :], new_sem(), left[h])
-        b.start()
-        p1[i] += [a, b]
+    for h in range(2):
+        for slot in range(2):
+            looped(lambda b, h=h, slot=slot: near(h, slot, b))
+        looped(lambda b, h=h: far_on(h, b))
+        for slot in range(3):
+            looped(lambda b, h=h, slot=slot: share(h, slot, b, c))
+    pass_z(NB - 1)
+    collect(0, NB - 1)
+
+    def each_block(f):
+        @pl.loop(0, NB)
+        def _(b):
+            f(b)
+
+    groups = (2 * zl, 2 * zl + 1, fz, fz + 1)
+
+    def product(lhs, rhs):
+        return dot(lhs.reshape(ROWS, ROWS), rhs, ((1,), (0,)))
+
+    def own_part(h):
+        mine = block_rows(h, 0)[...]
+        for g in range(2):
+            acc[2 * h + g] = product(mine, kvg[groups[2 * h + g]])
+
+    def near_part(h):
+        @pl.loop(0, NB)
+        def _(b):
+            share(h, 0, b, 1 - c).wait_recv()
+            share(h, 1, b, 1 - c).wait_recv()
+
+        for slot in range(2):
+            lhs = hx[h, slot]
+            for g in range(2):
+                acc[2 * h + g] += product(lhs, kx[h, slot, g])
 
     p2 = {}
 
-    def chunk(i, k, low, size):
-        return acc.at[i, pl.ds(pl.multiple_of(64 * k + low, 32), size), :]
-
-    def p2_start(i):
-        h = 1 - axis1[jobs[i][0]]
-        for cp in p1[i][2:]:
-            cp.wait_recv()
-        acc[i] = acc[i] + (r_nbl[i].astype(F32) + r_nbr[i].astype(F32))
-        k2, kr, kl = (me[h] + 2) % 4, (me[h] + 1) % 4, (me[h] + 3) % 4
-        cps = [
-            rcopy(chunk(i, k2, 0, 32), q_rel.at[i, 0:32, :], new_sem(), right[h]),
-            rcopy(chunk(i, k2, 32, 32), q_rel.at[i, 32:64, :], new_sem(), left[h]),
-            rcopy(chunk(i, kr, 32, 32), q_nbl.at[i, 32:64, :], new_sem(), right[h]),
-            rcopy(chunk(i, kl, 0, 32), q_nbr.at[i, 0:32, :], new_sem(), left[h]),
-        ]
-        for cp in cps:
-            cp.start()
-        p2[i] = cps
-
-    def p2_relay(i):
-        h = 1 - axis1[jobs[i][0]]
-        kr, kl = (me[h] + 1) % 4, (me[h] + 3) % 4
-        p2[i][0].wait_recv()
-        q_relay[i, 0:32, :] = chunk(i, kr, 0, 32)[...] + q_rel[i, 0:32, :]
-        a = rcopy(q_relay.at[i, 0:32, :], q_nbl.at[i, 0:32, :], new_sem(), right[h])
-        a.start()
-        p2[i][1].wait_recv()
-        q_relay[i, 32:64, :] = chunk(i, kl, 32, 32)[...] + q_rel[i, 32:64, :]
-        b = rcopy(q_relay.at[i, 32:64, :], q_nbr.at[i, 32:64, :], new_sem(), left[h])
-        b.start()
-        p2[i] += [a, b]
-
-    fin_send = new_sem(8)
-    fin_recv = new_sem(8)
-
-    def fin_copy(t, s, source, to):
-        rows = pl.ds(64 * s, 64)
+    def chunk(i, k):
+        return acc[i, pl.ds(pl.multiple_of(128 * k, 128), 128), :]
+
+    def far_part(h):
+        @pl.loop(0, NB)
+        def _(b):
+            share(h, 2, b, 1 - c).wait_recv()
+
+        lhs = hx[h, 2]
+        o = 1 - h
+        k2, kr, kl = (me[o] + 2) % 4, (me[o] + 1) % 4, (me[o] + 3) % 4
+        for g in range(2):
+            i = 2 * h + g
+            acc[i] += product(lhs, kx[h, 2, g])
+            cps = []
+            for ref, src, dst, to in (
+                (s_far, k2, q_far, across[o]), (s_rt, kr, q_nbl, right[o]), (s_lt, kl, q_nbr, left[o]),
+            ):
+                ref[i] = chunk(i, src).astype(BF16)
+                cp = rcopy(ref.at[i], dst.at[i], new_sem(), to)
+                cp.start()
+                cps.append(cp)
+            p2[i] = cps
+
+    fin_send = new_sem(4)
+    fin_recv = new_sem(4)
+
+    def fin_copy(i, source, to):
         return pltpu.make_async_remote_copy(
-            src_ref=z_acc.at[t, rows, :], dst_ref=r_fin.at[source, rows, :],
-            send_sem=snd.at[fin_send + 2 * t + s], recv_sem=rcv.at[fin_recv + 2 * source + s],
+            src_ref=z_acc.at[i], dst_ref=r_fin.at[source],
+            send_sem=snd.at[fin_send + i], recv_sem=rcv.at[fin_recv + source],
             device_id=to, device_id_type=MESH,
         )
 
     def p3_start(i):
-        t, s = jobs[i]
-        h = 1 - axis1[t]
-        for cp in p2[i][2:]:
+        t = groups[i]
+        for cp in p2[i]:
             cp.wait_recv()
-        rows = pl.ds(64 * s, 64)
-        z_acc[t, rows, :] = chunk(i, me[h], 0, 64)[...] + (q_nbl[i] + q_nbr[i])
+        near_sum = q_nbl[i].astype(F32) + q_nbr[i].astype(F32)
+        z_acc[i] = (chunk(i, me[1 - i // 2]) + q_far[i].astype(F32)) + near_sum
         local = (zh == j) & (j == t)
-        cp = fin_copy(t, s, zh, dev(j, y, x, t))
+        cp = fin_copy(i, zh, dev(j, y, x, t))
 
         @pl.when(local)
         def _():
-            r_fin[zh, rows, :] = z_acc[t, rows, :]
+            r_fin[zh] = z_acc[i]
 
         @pl.when(jnp.logical_not(local))
         def _():
@@ -401,10 +437,6 @@
             @pl.when(jnp.logical_not(local))
             def _():
                 cp.wait_send()
-
-    def both(f, n):
-        f(2 * n)
-        f(2 * n + 1)
 
     def hidden_grad(first, last):
         @pl.loop(first, last)
@@ -416,42 +448,26 @@
                 total = total + part.astype(BF16).astype(F32)
             hg[:, cols] = total.astype(BF16)
 
-    both(p1_far, 0)
-    both(p1_direct, 0)
-    both(p1_far, 1)
-    both(p1_own, 0)
-    both(p1_relay, 0)
-    both(p1_direct, 1)
-    both(p1_far, 2)
-    both(p1_own, 1)
-    both(p1_relay, 1)
-    both(p1_direct, 2)
-    both(p2_start, 0)
-    both(p1_far, 3)
-    both(p1_relay, 2)
-    both(p2_relay, 0)
-    both(p1_direct, 3)
-    both(p1_own, 2)
-    both(p1_own, 3)
-    both(p2_start, 1)
-    both(p3_start, 0)
-    both(p1_relay, 3)
-    both(p2_relay, 1)
-    hidden_grad(0, 3)
-    both(p2_start, 2)
-    both(p3_start, 1)
-    both(p2_relay, 2)
-    hidden_grad(3, 6)
-    both(p2_start, 3)
-    both(p3_start, 2)
-    both(p2_relay, 3)
-    hidden_grad(6, 8)
-    both(p3_start, 3)
+    each_block(lambda b: grad_copy(pj, b, kp_sem, partner).wait_recv())
+    own_part(0)
+    each_block(lambda b: collect(1, b))
+    for cp in h_near + h_far:
+        cp.wait_recv()
+    near_part(0)
+    far_part(0)
+    each_block(lambda b: grad_copy(tp, b, kf_sem, partner).wait_recv())
+    own_part(1)
+    near_part(1)
+    far_part(1)
+    p3_start(0)
+    p3_start(1)
+    p3_start(2)
+    p3_start(3)
+    hidden_grad(0, 8)
     for k in range(4):
         @pl.when(jnp.logical_not((zh == j) & (zh == k)))
         def _():
-            for s in range(2):
-                fin_copy(k, s, k, dev(k, y, x, zh)).wait_recv()
+            fin_copy(k, k, dev(k, y, x, zh)).wait_recv()
 
     wg_out[...] = (r_fin[0] + r_fin[1]) + (r_fin[2] + r_fin[3])
     finish()
@@ -483,15 +499,15 @@
         in_specs=[pl.BlockSpec(memory_space=pltpu.SMEM), vmem, any_, any_, any_, any_],
         out_specs=(vmem, vmem, vmem),
         scratch_shapes=[
-            vm((ROWS, KD), BF16), vm((KD, ROWS), BF16), vm((4, KD, KC), BF16),
+            vm((ROWS, KD), BF16), vm((4, 4, 128, ROWS), BF16), vm((4, KD, KC), BF16),
             vm((ROWS, NH * HD), BF16), vm((ROWS, NH * HD), BF16),
             vm((ROWS, KC), F32), vm((ROWS, KC), F32), vm((ROWS, KC), F32), vm((ROWS, KC), F32),
             vm((ROWS, KC), F32), vm((ROWS, KC), F32), vm((ROWS, KC), F32),
             vm((4, ROWS, KC), BF16),
-            vm((8, 256, KC), BF16), vm((8, 256, KC), BF16), vm((8, 256, KC), BF16),
-            vm((8, 128, KC), F32), vm((8, 128, KC), F32), vm((8, 256, KC), F32),
-            vm((8, 256, KC), BF16), vm((8, 256, KC), BF16), vm((8, 256, KC), BF16),
-            vm((8, 64, KC), F32), vm((8, 64, KC), F32), vm((8, 64, KC), F32), vm((8, 64, KC), F32),
+            vm((2, 3, 4, 128, ROWS), BF16),
+            vm((2, 3, 2, ROWS, KC), BF16), vm((4, ROWS, KC), F32),
+            vm((4, 128, KC), BF16), vm((4, 128, KC), BF16), vm((4, 128, KC), BF16),
+            vm((4, 128, KC), BF16), vm((4, 128, KC), BF16), vm((4, 128, KC), BF16),
             vm((4, 128, KC), F32), vm((4, 128, KC), F32),
             pltpu.SemaphoreType.DMA((N_LOC,)),
             pltpu.SemaphoreType.DMA((N_SEM,)),

time: 94.2 us -> 86.7 us (0.920)
  Pallas kernels: 92.8 us -> 85.3 us
    pallas_call x1, Pallas kernels: 91.1 us -> 83.5 us  [on_device(): pl.pallas_call(kernel, out_shape=tuple((vm(*r) for r in results)), in_spe...]
where the time goes in v3:
time: 86.7 us; the launch traced here: 86.5 us
  Pallas kernels  85.3 us (98%)
  between operations  1.29 us (1%)
    pallas_call x1, Pallas kernels, on_device(): pl.pallas_call(kernel, out_shape=tuple((vm(*r) for r in results)), in_spe...  83.5 us

profile of v3, /device:TPU:1, one launch (start us, length us, event | category | flops | bytes accessed | tf_op | source)
XLA Modules:
  0.0 86.5 jit_solution(3542942857175905365)
XLA Ops:
  1.3 83.5 %fused_step.1 = (bf16[512,1024]{1,0:T(8,128)(2,1)S(1)}, bf16[512,2048]{1,0:T(8,128)(2,1)S(1)}, f32[128,256]{1,0:T(8,128)S(1)}) custom-call(s32[1]{0:T(128)S(6)} %copy.9.live_ref, s32[4,128]{1,0:T(4,128)} %bitcast.1, bf16[512,2048]{1,0:T(8,128)(2,1)} %hid_hbm.1, bf16[8192,256]{1,0:T(8,128)(2,1)} %w_hbm.1, bf16[512,1024]{1,0:T(8,128)(2,1)} %q_hbm.1, ...), custom_call_target="tpu_custom_call" | custom-call | tf_op jit(solution)/shard_map/fused_step/pallas_call | solution.py:496
  84.8 1.7 %leave.1 = (bf16[512,1024]{1,0:T(8,128)(2,1)}, bf16[512,2048]{1,0:T(8,128)(2,1)}, f32[128,256]{1,0:T(8,128)}) custom-call(bf16[512,1024]{1,0:T(8,128)(2,1)S(1)} %get-tuple-element.6.qg, bf16[512,2048]{1,0:T(8,128)(2,1)S(1)} %get-tuple-element.7.hg, f32[128,256]{1,0:T(8,128)S(1)} %get-tuple-element.8.wg), custom_call_target="tpu_custom_call" | custom-call | tf_op jit(solution)/shard_map/leave/pallas_call | solution.py:521

commit v4 on v3

--- a/solution.py
+++ b/solution.py
@@ -7,6 +7,7 @@
 
 BF16 = jnp.bfloat16
 F32 = jnp.float32
+I16 = jnp.int16
 HD = 128
 ROWS = 512
 NB = 4
@@ -20,13 +21,25 @@
     return lax.dot_general(a, b, (dims, ((), ())), preferred_element_type=F32)
 
 
+def code(v):
+    top = jnp.max(jnp.abs(v), axis=0, keepdims=True)
+    inv = jnp.where(top > 0.0, 1.0 / top, 0.0)
+    n = v * inv * 32767.0
+    n = n + jnp.where(n >= 0.0, 0.5, -0.5)
+    return n.astype(jnp.int32).astype(jnp.int16), jnp.broadcast_to(top, (8, KC))
+
+
+def decode(n, top):
+    return n.astype(jnp.int32).astype(F32) * (1.0 / 32767.0) * top[0:1, :]
+
+
 def kernel(
     live_ref, start_ref, hid_hbm, w_hbm, q_hbm, g_hbm,
     qg, hg, wg_out,
     hid, hid_t, wts, qv, gv,
     own, pp, pf, ff, r_pp, r_pf, r_z, kvg,
-    hx, kx, acc, s_far, s_rt, s_lt, q_far, q_nbl, q_nbr,
-    z_acc, r_fin,
+    hx, kx, acc, s_far, s_rt, s_lt, q_far, q_nbl, q_nbr, s_t, q_t,
+    z_q, z_t, r_fin, r_ft,
     loc, snd, rcv,
 ):
     counter = [0, 0]
@@ -112,19 +125,22 @@
     own_case = jnp.where(zh == j, 1, 0)
     pl.semaphore_wait(barrier, 19 - 2 * own_case)
 
-    quarter = KD // 8
-    piece_rows = quarter // 2
+    order = (0, 2, 1, 3)
+
+    def piece_row(h, n):
+        return 1024 * h + 512 * (me[h] % 2) + 128 * n
+
     cp_z = {}
     for k in range(2):
         cd = (1 - c) if k == 0 else c
         td = fz + cd
-        for n in range(2):
+        for n in order:
             for h in range(2):
                 to = ((pair_other, pair_same), (oth_other, oth_same))[h][k]
-                off = 1024 * h + quarter * me[h] + piece_rows * n
+                off = piece_row(h, n)
                 cp = rcopy(
-                    w_hbm.at[pl.ds(KD * td + off, piece_rows), :],
-                    wts.at[j, pl.ds(off, piece_rows), :], new_sem(), to,
+                    w_hbm.at[pl.ds(KD * td + off, 128), :],
+                    wts.at[j, pl.ds(off, 128), :], new_sem(), to,
                 )
                 cp.start()
                 cp_z[k, n, h] = cp
@@ -146,42 +162,16 @@
             ref[rows, :] = value
         return store
 
-    ring = {}
-
-    def ring_near(k):
-        ts = (tp, tf)[k]
-        for n in range(2):
+    far = {0: [], 1: []}
+
+    def ring(k):
+        for n in order:
             for h in range(2):
                 cp_z[k, n, h].wait_recv()
-                sems = [new_sem() for _ in range(4)]
-
-                def piece(origin, lo, size, h=h, ts=ts, n=n):
-                    off = 1024 * h + quarter * origin + piece_rows * n + lo
-                    return wts.at[ts, pl.ds(off, size), :]
-
-                mine = piece(me[h], 0, piece_rows)
-                a = rcopy(mine, mine, sems[0], right[h])
-                b = rcopy(mine, mine, sems[1], left[h])
-                a.start()
-                b.start()
-                ring[k, n, h] = (a, b, sems, piece)
-
-    far = {0: [], 1: []}
-
-    def ring_far(k):
-        half = piece_rows // 2
-        for n in range(2):
-            for h in range(2):
-                a, b, sems, piece = ring[k, n, h]
-                a.wait_recv()
-                first = piece((me[h] + 3) % 4, 0, half)
-                fa = rcopy(first, first, sems[2], right[h])
-                fa.start()
-                b.wait_recv()
-                second = piece((me[h] + 1) % 4, half, half)
-                fb = rcopy(second, second, sems[3], left[h])
-                fb.start()
-                far[k] += [fa, fb]
+                ref = wts.at[(tp, tf)[k], pl.ds(piece_row(h, n), 128), :]
+                cp = rcopy(ref, ref, new_sem(), right[h] if n < 2 else left[h])
+                cp.start()
+                far[k].append(cp)
 
     cp_hid.wait()
 
@@ -213,17 +203,15 @@
             h_far.append(cp)
 
     send_hidden(0, 2)
-    ring_near(0)
+    ring(0)
     cp_own.wait()
     proj(j, to_ref(own))
-    ring_near(1)
-    ring_far(0)
+    ring(1)
     cp_pw.wait_recv()
     proj(pj, to_ref(pp))
     cp_pp = rcopy(pp, r_pp, new_sem(), partner)
     cp_pp.start()
 
-    ring_far(1)
     send_hidden_rest()
 
     for cp in far[0]:
@@ -396,47 +384,54 @@
             i = 2 * h + g
             acc[i] += product(lhs, kx[h, 2, g])
             cps = []
-            for ref, src, dst, to in (
+            for n, (ref, src, dst, to) in enumerate((
                 (s_far, k2, q_far, across[o]), (s_rt, kr, q_nbl, right[o]), (s_lt, kl, q_nbr, left[o]),
-            ):
-                ref[i] = chunk(i, src).astype(BF16)
-                cp = rcopy(ref.at[i], dst.at[i], new_sem(), to)
-                cp.start()
-                cps.append(cp)
+            )):
+                ref[i], s_t[n, i] = code(chunk(i, src))
+                for a, b in ((s_t.at[n, i], q_t.at[n, i]), (ref.at[i], dst.at[i])):
+                    cp = rcopy(a, b, new_sem(), to)
+                    cp.start()
+                    cps.append(cp)
             p2[i] = cps
 
-    fin_send = new_sem(4)
-    fin_recv = new_sem(4)
-
-    def fin_copy(i, source, to):
-        return pltpu.make_async_remote_copy(
-            src_ref=z_acc.at[i], dst_ref=r_fin.at[source],
-            send_sem=snd.at[fin_send + i], recv_sem=rcv.at[fin_recv + source],
-            device_id=to, device_id_type=MESH,
-        )
+    fin_send = new_sem(8)
+    fin_recv = new_sem(8)
+
+    def fin_copies(i, source, to):
+        return [
+            pltpu.make_async_remote_copy(
+                src_ref=src.at[i], dst_ref=dst.at[source],
+                send_sem=snd.at[fin_send + 4 * n + i], recv_sem=rcv.at[fin_recv + 4 * n + source],
+                device_id=to, device_id_type=MESH,
+            )
+            for n, (src, dst) in enumerate(((z_t, r_ft), (z_q, r_fin)))
+        ]
 
     def p3_start(i):
         t = groups[i]
         for cp in p2[i]:
             cp.wait_recv()
-        near_sum = q_nbl[i].astype(F32) + q_nbr[i].astype(F32)
-        z_acc[i] = (chunk(i, me[1 - i // 2]) + q_far[i].astype(F32)) + near_sum
+        near_sum = decode(q_nbl[i], q_t[1, i]) + decode(q_nbr[i], q_t[2, i])
+        z_q[i], z_t[i] = code((chunk(i, me[1 - i // 2]) + decode(q_far[i], q_t[0, i])) + near_sum)
         local = (zh == j) & (j == t)
-        cp = fin_copy(i, zh, dev(j, y, x, t))
+        cps = fin_copies(i, zh, dev(j, y, x, t))
 
         @pl.when(local)
         def _():
-            r_fin[zh] = z_acc[i]
+            r_fin[zh] = z_q[i]
+            r_ft[zh] = z_t[i]
 
         @pl.when(jnp.logical_not(local))
         def _():
-            cp.start()
+            for cp in cps:
+                cp.start()
 
         @sent.append
         def _():
             @pl.when(jnp.logical_not(local))
             def _():
-                cp.wait_send()
+                for cp in cps:
+                    cp.wait_send()
 
     def hidden_grad(first, last):
         @pl.loop(first, last)
@@ -461,15 +456,18 @@
     far_part(1)
     p3_start(0)
     p3_start(1)
+    hidden_grad(0, 1)
     p3_start(2)
     p3_start(3)
-    hidden_grad(0, 8)
+    hidden_grad(1, 8)
     for k in range(4):
         @pl.when(jnp.logical_not((zh == j) & (zh == k)))
         def _():
-            fin_copy(k, k, dev(k, y, x, zh)).wait_recv()
-
-    wg_out[...] = (r_fin[0] + r_fin[1]) + (r_fin[2] + r_fin[3])
+            for cp in fin_copies(k, k, dev(k, y, x, zh)):
+                cp.wait_recv()
+
+    parts = [decode(r_fin[k], r_ft[k]) for k in range(4)]
+    wg_out[...] = (parts[0] + parts[1]) + (parts[2] + parts[3])
     finish()
 
 
@@ -506,9 +504,10 @@
             vm((4, ROWS, KC), BF16),
             vm((2, 3, 4, 128, ROWS), BF16),
             vm((2, 3, 2, ROWS, KC), BF16), vm((4, ROWS, KC), F32),
-            vm((4, 128, KC), BF16), vm((4, 128, KC), BF16), vm((4, 128, KC), BF16),
-            vm((4, 128, KC), BF16), vm((4, 128, KC), BF16), vm((4, 128, KC), BF16),
-            vm((4, 128, KC), F32), vm((4, 128, KC), F32),
+            vm((4, 128, KC), I16), vm((4, 128, KC), I16), vm((4, 128, KC), I16),
+            vm((4, 128, KC), I16), vm((4, 128, KC), I16), vm((4, 128, KC), I16),
+            vm((3, 4, 8, KC), F32), vm((3, 4, 8, KC), F32),
+            vm((4, 128, KC), I16), vm((4, 8, KC), F32), vm((4, 128, KC), I16), vm((4, 8, KC), F32),
             pltpu.SemaphoreType.DMA((N_LOC,)),
             pltpu.SemaphoreType.DMA((N_SEM,)),
             pltpu.SemaphoreType.DMA((N_SEM,)),

time: 86.7 us -> 83.6 us (0.964)
  Pallas kernels: 85.3 us -> 82.2 us
    pallas_call x1, Pallas kernels: 83.5 us -> 80.4 us  [on_device(): pl.pallas_call(kernel, out_shape=tuple((vm(*r) for r in results)), in_spe...]
where the time goes in v4:
time: 83.6 us; the launch traced here: 83.4 us
  Pallas kernels  82.2 us (98%)
  between operations  1.29 us (2%)
    pallas_call x1, Pallas kernels, on_device(): pl.pallas_call(kernel, out_shape=tuple((vm(*r) for r in results)), in_spe...  80.4 us
    pallas_call x1, Pallas kernels, on_device(): pl.pallas_call(leave, out_shape=tuple((jax.ShapeDtypeStruct(*r) for r in...  1.72 us

profile of v4, /device:TPU:1, one launch (start us, length us, event | category | flops | bytes accessed | tf_op | source)
XLA Modules:
  0.0 83.4 jit_solution(8361150519022973850)
XLA Ops:
  1.3 80.4 %fused_step.1 = (bf16[512,1024]{1,0:T(8,128)(2,1)S(1)}, bf16[512,2048]{1,0:T(8,128)(2,1)S(1)}, f32[128,256]{1,0:T(8,128)S(1)}) custom-call(s32[1]{0:T(128)S(6)} %copy.9.live_ref, s32[4,128]{1,0:T(4,128)} %bitcast.1, bf16[512,2048]{1,0:T(8,128)(2,1)} %hid_hbm.1, bf16[8192,256]{1,0:T(8,128)(2,1)} %w_hbm.1, bf16[512,1024]{1,0:T(8,128)(2,1)} %q_hbm.1, ...), custom_call_target="tpu_custom_call" | custom-call | tf_op jit(solution)/shard_map/fused_step/pallas_call | solution.py:494
  81.7 1.7 %leave.1 = (bf16[512,1024]{1,0:T(8,128)(2,1)}, bf16[512,2048]{1,0:T(8,128)(2,1)}, f32[128,256]{1,0:T(8,128)}) custom-call(bf16[512,1024]{1,0:T(8,128)(2,1)S(1)} %get-tuple-element.6.qg, bf16[512,2048]{1,0:T(8,128)(2,1)S(1)} %get-tuple-element.7.hg, f32[128,256]{1,0:T(8,128)S(1)} %get-tuple-element.8.wg), custom_call_target="tpu_custom_call" | custom-call | tf_op jit(solution)/shard_map/leave/pallas_call | solution.py:520

commit v5 on v4

--- a/solution.py
+++ b/solution.py
@@ -123,6 +123,16 @@
         def _():
             greet(dev(k, y, x, zh))
     own_case = jnp.where(zh == j, 1, 0)
+
+    def transpose(first, last):
+        @pl.loop(first, last)
+        def _(k):
+            for n in range(4):
+                cols = pl.ds(pl.multiple_of(512 * k + 128 * n, 128), 128)
+                hid_t[k, n] = hid[:, cols].T
+
+    cp_hid.wait()
+    transpose(0, 2)
     pl.semaphore_wait(barrier, 19 - 2 * own_case)
 
     order = (0, 2, 1, 3)
@@ -173,13 +183,7 @@
                 cp.start()
                 far[k].append(cp)
 
-    cp_hid.wait()
-
-    @pl.loop(0, 4)
-    def _(k):
-        for n in range(4):
-            cols = pl.ds(pl.multiple_of(512 * k + 128 * n, 128), 128)
-            hid_t[k, n] = hid[:, cols].T
+    transpose(2, 4)
 
     def block_rows(h, step):
         dest = (me[h] + step) % 4
@@ -207,12 +211,11 @@
     cp_own.wait()
     proj(j, to_ref(own))
     ring(1)
+    send_hidden_rest()
     cp_pw.wait_recv()
     proj(pj, to_ref(pp))
     cp_pp = rcopy(pp, r_pp, new_sem(), partner)
     cp_pp.start()
-
-    send_hidden_rest()
 
     for cp in far[0]:
         cp.wait_recv()
@@ -327,7 +330,6 @@
         @pl.when(b >= 1)
         def _():
             pass_z(b - 1)
-            collect(0, b - 1)
 
     looped(lambda b: grad_copy(j, b, kz_sem, pair_same))
     looped(lambda b: grad_copy(j, b, kp_sem, partner))
@@ -339,7 +341,6 @@
         for slot in range(3):
             looped(lambda b, h=h, slot=slot: share(h, slot, b, c))
     pass_z(NB - 1)
-    collect(0, NB - 1)
 
     def each_block(f):
         @pl.loop(0, NB)
@@ -445,13 +446,21 @@
 
     each_block(lambda b: grad_copy(pj, b, kp_sem, partner).wait_recv())
     own_part(0)
-    each_block(lambda b: collect(1, b))
-    for cp in h_near + h_far:
+    each_block(lambda b: collect(0, b))
+    each_block(lambda b: grad_copy(tp, b, kf_sem, partner).wait_recv())
+    own_part(1)
+
+    @pl.loop(0, NB - 1)
+    def _(b):
+        collect(1, b)
+
+    for cp in h_near:
         cp.wait_recv()
     near_part(0)
+    collect(1, NB - 1)
+    for cp in h_far:
+        cp.wait_recv()
     far_part(0)
-    each_block(lambda b: grad_copy(tp, b, kf_sem, partner).wait_recv())
-    own_part(1)
     near_part(1)
     far_part(1)
     p3_start(0)

time: 83.6 us -> 81.2 us (0.971)
  Pallas kernels: 82.2 us -> 79.8 us
    pallas_call x1, Pallas kernels: 80.4 us -> 78.1 us  [on_device(): pl.pallas_call(kernel, out_shape=tuple((vm(*r) for r in results)), in_spe...]
where the time goes in v5:
time: 81.2 us; the launch traced here: 81.1 us
  Pallas kernels  79.8 us (98%)
  between operations  1.29 us (2%)
    pallas_call x1, Pallas kernels, on_device(): pl.pallas_call(kernel, out_shape=tuple((vm(*r) for r in results)), in_spe...  78.1 us
    pallas_call x1, Pallas kernels, on_device(): pl.pallas_call(leave, out_shape=tuple((jax.ShapeDtypeStruct(*r) for r in...  1.72 us

profile of v5, /device:TPU:1, one launch (start us, length us, event | category | flops | bytes accessed | tf_op | source)
XLA Modules:
  0.0 81.1 jit_solution(13799261439096105957)
XLA Ops:
  1.3 78.1 %fused_step.1 = (bf16[512,1024]{1,0:T(8,128)(2,1)S(1)}, bf16[512,2048]{1,0:T(8,128)(2,1)S(1)}, f32[128,256]{1,0:T(8,128)S(1)}) custom-call(s32[1]{0:T(128)S(6)} %copy.9.live_ref, s32[4,128]{1,0:T(4,128)} %bitcast.1, bf16[512,2048]{1,0:T(8,128)(2,1)} %hid_hbm.1, bf16[8192,256]{1,0:T(8,128)(2,1)} %w_hbm.1, bf16[512,1024]{1,0:T(8,128)(2,1)} %q_hbm.1, ...), custom_call_target="tpu_custom_call" | custom-call | tf_op jit(solution)/shard_map/fused_step/pallas_call | solution.py:503
  79.4 1.7 %leave.1 = (bf16[512,1024]{1,0:T(8,128)(2,1)}, bf16[512,2048]{1,0:T(8,128)(2,1)}, f32[128,256]{1,0:T(8,128)}) custom-call(bf16[512,1024]{1,0:T(8,128)(2,1)S(1)} %get-tuple-element.6.qg, bf16[512,2048]{1,0:T(8,128)(2,1)S(1)} %get-tuple-element.7.hg, f32[128,256]{1,0:T(8,128)S(1)} %get-tuple-element.8.wg), custom_call_target="tpu_custom_call" | custom-call | tf_op jit(solution)/shard_map/leave/pallas_call | solution.py:529
